TPU v7x, 32 devices: a whole 2x2x4 slice. The times are simulated.
32 devices in a mesh: groups: 1, seq: 32 (over z, y, x, core).
Axes of the slice: x: 2, y: 2, z: 4, core: 2. Of those that a mesh axis runs over, the one named last changes fastest.
Arguments:
- q_gate: bfloat16 [4096, 4096], P(('groups', 'seq')), may hold values from -6 to 6
- values_in: bfloat16 [4096, 4096], P(('groups', 'seq')), may hold values from -6 to 6
- decay_rate: float32 [4096, 16], replicated, as said below
- residue: float32 [4096, 16], replicated, may hold values from -3 to 3
- skip_gain: float32 [4096], replicated, may hold values from 0.5 to 1.5
- out_weight: bfloat16 [4096, 2048], P('seq'), may hold values from -0.09375 to 0.09375
Outputs:
- mixed: bfloat16 [4096, 2048], P(('groups', 'seq'))
Inputs may be any that keep to these rules, and one draw needn't show every extreme that they name: `decay_rate`: every rate is positive and at most about 1/30.
All inputs are finite; a program needn't handle non-finite values.
Results may differ from a plain program's by a relative error of at most 0.0052.
Values may be sent and summed in bfloat16 or wider, within the bound.
A program may use at most 256 MiB of HBM per device.

v0:
```python
import jax
import jax.numpy as jnp
from jax import lax
from jax.sharding import PartitionSpec as P

ORDER = 16
BLOCK = 32


def entering(value, axis, join, neutral):
    count, mine = (lax.axis_size(axis), lax.axis_index(axis))
    pieces = jax.tree.map(lambda part: lax.all_gather(part, axis), value)
    running = jax.tree.map(
        lambda part, zero: jnp.full_like(part, 0) + jnp.asarray(zero, part.dtype), value, neutral
    )

    def hop(position, running):
        longer = join(running, jax.tree.map(lambda part: part[position], pieces))
        return jax.tree.map(lambda new, old: jnp.where(position < mine, new, old), longer, running)

    return lax.fori_loop(0, count - 1, hop, running)


def on_device(q_gate, values_in, decay_rate, residue, skip_gain, out_weight):
    tok_rows = q_gate.shape[0]
    width = q_gate.shape[1]
    block_count = tok_rows // BLOCK
    rate_modes = decay_rate.T
    mode_scale = jnp.sqrt(-jnp.expm1(-2.0 * rate_modes))
    mode_coef = residue.T * mode_scale
    position = jnp.arange(BLOCK, dtype=jnp.float32)
    tap_values = jnp.sum(
        mode_coef[None] * jnp.exp(-position[:, None, None] * rate_modes[None]), axis=1
    )
    tap_round = tap_values.astype(jnp.bfloat16)
    offsets = jnp.arange(BLOCK)[:, None] - jnp.arange(BLOCK)[None, :]
    selector = (
        (jnp.arange(BLOCK)[:, None, None] == offsets[None])
        .astype(jnp.bfloat16)
        .reshape(BLOCK, BLOCK * BLOCK)
    )
    toeplitz = jnp.dot(tap_round.T, selector, preferred_element_type=jnp.bfloat16).reshape(
        width, BLOCK, BLOCK
    )
    blocked = values_in.reshape(block_count, BLOCK, width)
    local_part = jnp.einsum("dts,nsd->ntd", toeplitz, blocked, preferred_element_type=jnp.float32)
    blocked_wide = blocked.astype(jnp.float32)
    end_weight = jnp.exp(-(BLOCK - 1 - position)[:, None, None] * rate_modes[None])
    block_ends = jnp.einsum(
        "tkd,ntd->nkd", end_weight, blocked_wide, precision=lax.Precision.HIGHEST
    )
    step_decay = jnp.exp(-BLOCK * rate_modes)

    def advance(carry_state, inflow):
        return (step_decay * carry_state + inflow, carry_state)

    end_state, starts_local = lax.scan(advance, jnp.zeros((ORDER, width), jnp.float32), block_ends)
    shard_decay = jnp.exp(-tok_rows * rate_modes)

    def combine_pairs(earlier, later):
        return (earlier[0] * later[0], earlier[1] * later[0] + later[1])

    identity = (jnp.ones_like(shard_decay), jnp.zeros_like(end_state))
    scanned = entering((shard_decay, end_state), "seq", combine_pairs, identity)
    incoming = scanned[1]
    block_index = jnp.arange(block_count, dtype=jnp.float32)
    starts = (
        starts_local
        + jnp.exp(-(BLOCK * block_index)[:, None, None] * rate_modes[None]) * incoming[None]
    )
    reach_table = mode_coef[None] * jnp.exp(-(position + 1.0)[:, None, None] * rate_modes[None])
    correction = jnp.einsum("tkd,nkd->ntd", reach_table, starts, precision=lax.Precision.HIGHEST)
    conv = (local_part + correction).reshape(tok_rows, width)
    gated = (
        q_gate.astype(jnp.float32) * (conv + skip_gain[None] * values_in.astype(jnp.float32))
    ).astype(jnp.bfloat16)
    weights = lax.all_gather(out_weight, "seq", axis=0, tiled=True)
    mixed = jnp.dot(gated, weights, preferred_element_type=jnp.float32)
    return mixed.astype(jnp.bfloat16)


def solution(mesh):
    in_specs = (
        P(("groups", "seq"), None),
        P(("groups", "seq"), None),
        P(),
        P(),
        P(),
        P("seq", None),
    )
    out_specs = P(("groups", "seq"), None)
    return jax.shard_map(
        on_device, mesh=mesh, in_specs=in_specs, out_specs=out_specs, check_vma=False
    )
```

profile of v0, /device:TPU:0, one launch (start us, length us, event | category | flops | bytes accessed | tf_op | source)
XLA Modules:
  0.0 299.8 jit_solution(8403443552745695005)
XLA Ops:
  6.5 1.9 multiply_exponential_fusion
  8.6 1.5 copy.31
  10.1 6.2 %copy.34 = bf16[4,32,4096]{1,0,2:T(4,128)(2,1)} copy(bf16[4,32,4096]{2,1,0:T(8,128)(2,1)} %bitcast.53) | data formatting | bytes 2097152 | tf_op jit(solution)/shard_map/reshape | solution.py:45
  16.3 34.1 %fusion.13 = f32[4,16,4096]{1,0,2:T(4,128)} fusion(bf16[4,32,4096]{1,0,2:T(4,128)(2,1)} %copy.34, f32[32]{0:T(128)S(1)} %subtract_negate_fusion, f32[16,4096]{0,1:T(8,128)S(1)} %copy.31), kind=kOutput, calls=%fused_computation.19 | convolution fusion | flops 102760448 | bytes 2359424 | tf_op jit(solution)/shard_map/tkd,ntd->nkd/dot_general | solution.py:49
  50.4 7.5 %copy.36 = f32[4,16,4096]{2,1,0:T(8,128)} copy(f32[4,16,4096]{1,0,2:T(4,128)} %fusion.13) | data formatting | bytes 2097152
  57.9 7.5 %while.27 = (s32[]{:T(128)}, f32[16,4096]{1,0:T(8,128)S(1)}, f32[4,16,4096]{2,1,0:T(8,128)}, f32[16,4096]{1,0:T(8,128)S(1)}, f32[4,16,4096]{2,1,0:T(8,128)}, /*index=5*/s32[]{:T(128)}, s32[]{:T(128)}) while((s32[]{:T(128)}, f32[16,4096]{1,0:T(8,128)S(1)}, f32[4,16,4096]{2,1,0:T(8,128)}, f32[16,4096]{1,0:T(8,128)S(1)}, ...), condition=%wide.region_2.3_spmd.clone, body=%wide.region_1.2_spmd.clone.sunk | while | flops 262147 | bytes 1572968 | solution.py:57
  67.0 2.0 copy.30
  68.9 25.7 %multiply_reduce_fusion = bf16[32,4096]{0,1:T(8,128)(2,1)} fusion(f32[16,4096]{0,1:T(8,128)S(1)} %copy.31, f32[32]{0:T(128)S(1)} %iota_negate_fusion, f32[16,4096]{0,1:T(8,128)} %copy.30), kind=kLoop, calls=%fused_computation.12 | loop fusion | flops 6160384 | bytes 786560 | tf_op jit(solution)/shard_map/reduce_sum | solution.py:32
  94.6 1.5 copy.32
  96.2 5.6 %fusion.20 = bf16[4096,32,32]{0,2,1:T(8,128)(2,1)} fusion(s32[32,32]{1,0:T(8,128)S(1)} %iota_subtract_fusion, bf16[32,4096]{1,0:T(8,128)(2,1)S(1)} %copy.32), kind=kOutput, calls=%fused_computation.26 | convolution fusion | flops 268468224 | bytes 8654848 | tf_op jit(solution)/shard_map/dot_general | solution.py:42
  101.7 44.1 %copy.33 = bf16[4096,32,32]{2,1,0:T(8,128)(2,1)} copy(bf16[4096,32,32]{0,2,1:T(8,128)(2,1)} %fusion.20) | data formatting | bytes 16777216 | tf_op jit(solution)/shard_map/dot_general | solution.py:42
  145.9 22.9 %fusion.24 = f32[4096,32,4]{1,2,0:T(4,128)} fusion(bf16[4096,32,32]{2,1,0:T(8,128)(2,1)} %copy.33, bf16[4,32,4096]{1,0,2:T(4,128)(2,1)} %copy.34), kind=kOutput, calls=%fused_computation.38 | convolution fusion | flops 33554432 | bytes 11534336 | tf_op jit(solution)/shard_map/dts,nsd->ntd/dot_general | solution.py:46
  168.8 39.5 %while.28 = (s32[]{:T(128)}, f32[16,4096]{1,0:T(8,128)S(1)}, s32[]{:T(128)}, f32[32,16,4096]{2,1,0:T(8,128)}, f32[32,16,4096]{2,1,0:T(8,128)}, /*index=5*/s32[]{:T(128)}, s32[]{:T(128)}) while((s32[]{:T(128)}, f32[16,4096]{1,0:T(8,128)S(1)}, s32[]{:T(128)}, f32[32,16,4096]{2,1,0:T(8,128)}, f32[32,16,4096]{2,1,0:T(8,128)}, ...), condition=%wide.region_4.5_spmd.clone, body=%wide.region_3.4_spmd.clone.sunk | while | flops 262148 | bytes 1048685 | solution.py:21
  177.7 1.3 fusion.35
  179.0 1.3 fusion.35
  190.5 1.3 fusion.35
  199.4 1.3 fusion.35
  208.3 2.5 multiply_add_fusion
  210.9 6.9 %copy.37 = f32[4,16,4096]{1,0,2:T(4,128)} copy(f32[4,16,4096]{2,1,0:T(8,128)} %multiply_add_fusion) | data formatting | bytes 2097152 | tf_op jit(solution)/shard_map/add | solution.py:68
  217.7 47.3 %bitcast_add_fusion.2 = f32[4,32,4096]{1,0,2:T(4,128)} fusion(f32[4096,32,4]{1,2,0:T(4,128)} %fusion.24, f32[4,16,4096]{1,0,2:T(4,128)} %copy.37, f32[32]{0:T(128)S(1)} %add_negate_fusion, f32[16,4096]{0,1:T(8,128)S(1)} %copy.31, f32[16,4096]{0,1:T(8,128)} %copy.30), kind=kOutput, calls=%fused_computation.18 | convolution fusion | flops 105381888 | bytes 5767296 | tf_op jit(solution)/shard_map/tkd,nkd->ntd/dot_general | solution.py:72
  265.1 7.0 %copy.38 = f32[4,32,4096]{2,1,0:T(8,128)S(1)} copy(f32[4,32,4096]{1,0,2:T(4,128)} %bitcast_add_fusion.2) | data formatting | bytes 4194304 | tf_op jit(solution)/shard_map/add | solution.py:73
  272.1 2.2 fusion.19
  274.3 10.2 %all-gather.6.cloned.1.call-done = bf16[4096,2048]{1,0:T(8,128)(2,1)} async-done(((bf16[128,2048]{1,0:T(8,128)(2,1)}), bf16[4096,2048]{1,0:T(8,128)(2,1)}) %all-gather.6.cloned.1.call-update) | async-done | bytes 16777232 | tf_op jit(solution)/shard_map/all_gather | solution.py:77
  284.4 8.9 %convolution_convert_fusion = bf16[128,2048]{1,0:T(8,128)(2,1)} fusion(bf16[128,4096]{1,0:T(8,128)(2,1)S(1)} %fusion.19, bf16[4096,2048]{1,0:T(8,128)(2,1)} %all-gather.6.cloned.1.call-done), kind=kOutput, calls=%fused_computation.20 | convolution fusion | flops 2147745792 | bytes 18350080 | tf_op jit(solution)/shard_map/dot_general | solution.py:78
  (57 shorter events, 42.7 us)
Async XLA Ops:
  6.5 162.2 %all-gather.8.cloned.1.call-start = ((), (), s32[]{:S(2)}) async-start(), calls=%async_computation.1 | async-start | bytes 8650752 | tf_op jit(solution)/shard_map/all_gather | solution.py:12
  8.5 160.3 %all-gather.10.cloned.1.call-start = ((), (), s32[]{:S(2)}) async-start(), calls=%async_computation.2 | async-start | bytes 8650752 | tf_op jit(solution)/shard_map/all_gather | solution.py:12
  65.4 0.7 copy-start
  66.2 218.3 %all-gather.6.cloned.1.call-start = ((), (), s32[]{:S(2)}) async-start(), calls=%async_computation | async-start | bytes 17301504 | tf_op jit(solution)/shard_map/all_gather | solution.py:77
  145.9 62.4 %copy-start.1 = (f32[4096,16]{0,1:T(8,128)S(1)}, f32[4096,16]{0,1:T(8,128)}, u32[]{:S(2)}) copy-start(f32[4096,16]{0,1:T(8,128)} %param.12) | copy-start | bytes 786436
  265.1 7.0 %copy-start.2 = (f32[4096]{0:T(1024)S(1)}, f32[4096]{0:T(1024)}, u32[]{:S(2)}) copy-start(f32[4096]{0:T(1024)} %param.14) | copy-start | bytes 49156
Sparse Core Ops, SparseCore 0:
  10.2 79.7 all-gather.7
  92.9 75.6 all-gather.9
  171.4 112.9 all-gather.5
where the time goes:
time: 302 us; the launch traced here: 300 us
  matrix products  119 us (39%)
  other arithmetic  78.6 us (26%)
  local copies, waits for them, and re-layouts  77.5 us (26%)
  between operations  13.2 us (4%)
  waiting for transfers between devices  10.7 us (4%)
    dot_general x1, matrix products, on_device(): jnp.einsum('tkd,nkd->ntd', reach_table, starts, precision=lax.Precision.H...  47.3 us
    dot_general x1, local copies, waits for them, and re-layouts, on_device(): jnp.dot(tap_round.T, selector, preferred_element_type=jnp.bfloat16)  44.1 us
    select_n x31, other arithmetic, hop(): jnp.where(position < mine, new, old)  38.9 us
    dot_general x1, matrix products, on_device(): jnp.einsum('tkd,ntd->nkd', end_weight, blocked_wide, precision=lax.Precis...  34.1 us
    reduce_sum x1, other arithmetic, on_device(): jnp.sum(mode_coef[None] * jnp.exp(-position[:, None, None] * rate_modes[N...  25.7 us
    dot_general x1, matrix products, on_device(): jnp.einsum('dts,nsd->ntd', toeplitz, blocked, preferred_element_type=jnp....  22.9 us
    all_gather x1, waiting for transfers between devices, on_device(): weights = lax.all_gather(out_weight, 'seq', axis=0, tiled=True)  10.2 us
    dot_general x1, matrix products, on_device(): mixed = jnp.dot(gated, weights, preferred_element_type=jnp.float32)  8.9 us
  transfers between devices with their start and end apart: 3, of which 1 were waited for; matrix products, arithmetic and copies ran while one was open for 88% of the time, Pallas kernels for 0%

commit v1 on v0

--- a/solution.py
+++ b/solution.py
@@ -1,3 +1,4 @@
+import functools
 import jax
 import jax.numpy as jnp
 from jax import lax
@@ -5,6 +6,16 @@
 
 ORDER = 16
 BLOCK = 32
+
+
+def fit_edges_on(vec, axis_tag):
+    step_out = jnp.concatenate(
+        lax.all_to_all(jnp.stack(lax.psum(1, axis_tag) * [vec]), axis_tag, 0, 0), axis=0
+    )
+    return step_out
+
+
+scan_patches_all = functools.partial(fit_edges_on, axis_tag="seq")
 
 
 def entering(value, axis, join, neutral):
@@ -74,7 +85,7 @@
     gated = (
         q_gate.astype(jnp.float32) * (conv + skip_gain[None] * values_in.astype(jnp.float32))
     ).astype(jnp.bfloat16)
-    weights = lax.all_gather(out_weight, "seq", axis=0, tiled=True)
+    weights = scan_patches_all(out_weight)
     mixed = jnp.dot(gated, weights, preferred_element_type=jnp.float32)
     return mixed.astype(jnp.bfloat16)
 

time: 302 us -> 511 us (1.69)
  waiting for transfers between devices: 10.7 us -> 206 us
  starting transfers between devices: 0.27 us -> 7.62 us
  local copies, waits for them, and re-layouts: 77.5 us -> 83.6 us
    all_gather x2, waiting for transfers between devices: 0.01 us -> 144 us  [entering(): pieces = jax.tree.map(lambda part: lax.all_gather(part, axis), value)]
    all_to_all x0 -> x1, waiting for transfers between devices: none -> 62.8 us  [fit_edges_on(): lax.all_to_all(jnp.stack(lax.psum(1, axis_tag) * [vec]), axis_tag, 0, 0)]
    all_gather x1 -> x0, waiting for transfers between devices: 10.2 us -> none  [on_device(): weights = lax.all_gather(out_weight, 'seq', axis=0, tiled=True)]
    all_to_all x0 -> x1, starting transfers between devices: none -> 7.57 us  [fit_edges_on(): lax.all_to_all(jnp.stack(lax.psum(1, axis_tag) * [vec]), axis_tag, 0, 0)]
    another operation x0 -> x1, local copies, waits for them, and re-layouts: none -> 6.04 us  [fit_edges_on(): jnp.stack(lax.psum(1, axis_tag) * [vec])]
  transfers between devices with their start and end apart: 3 -> 3, of which waited for: 1 -> 2; matrix products, arithmetic and copies ran while one was open for 88% -> 53% of each run, Pallas kernels for 0% -> 0%
where the time goes in v1:
time: 511 us; the launch traced here: 509 us
  waiting for transfers between devices  206 us (40%)
  matrix products  119 us (23%)
  local copies, waits for them, and re-layouts  83.6 us (16%)
  other arithmetic  78.4 us (15%)
  between operations  13.5 us (3%)
  starting transfers between devices  7.62 us (1%)
    all_gather x2, waiting for transfers between devices, entering(): pieces = jax.tree.map(lambda part: lax.all_gather(part, axis), value)  144 us
    all_to_all x1, waiting for transfers between devices, fit_edges_on(): lax.all_to_all(jnp.stack(lax.psum(1, axis_tag) * [vec]), axis_tag, 0, 0)  62.8 us
    dot_general x1, matrix products, on_device(): jnp.einsum('tkd,nkd->ntd', reach_table, starts, precision=lax.Precision.H...  47.3 us
    dot_general x1, local copies, waits for them, and re-layouts, on_device(): jnp.dot(tap_round.T, selector, preferred_element_type=jnp.bfloat16)  44.1 us
    select_n x31, other arithmetic, hop(): jnp.where(position < mine, new, old)  38.7 us
    dot_general x1, matrix products, on_device(): jnp.einsum('tkd,ntd->nkd', end_weight, blocked_wide, precision=lax.Precis...  34.1 us
    reduce_sum x1, other arithmetic, on_device(): jnp.sum(mode_coef[None] * jnp.exp(-position[:, None, None] * rate_modes[N...  25.7 us
    dot_general x1, matrix products, on_device(): jnp.einsum('dts,nsd->ntd', toeplitz, blocked, preferred_element_type=jnp....  22.7 us
  transfers between devices with their start and end apart: 3, of which 2 were waited for; matrix products, arithmetic and copies ran while one was open for 53% of the time, Pallas kernels for 0%

profile of v1, /device:TPU:0, one launch (start us, length us, event | category | flops | bytes accessed | tf_op | source)
XLA Modules:
  0.0 508.8 jit_solution(3938349166019980672)
XLA Ops:
  6.5 1.9 multiply_exponential_fusion
  8.6 1.5 copy.31
  10.1 6.2 %copy.34 = bf16[4,32,4096]{1,0,2:T(4,128)(2,1)} copy(bf16[4,32,4096]{2,1,0:T(8,128)(2,1)} %bitcast.54) | data formatting | bytes 2097152 | tf_op jit(solution)/shard_map/reshape | solution.py:56
  16.3 34.1 %fusion.13 = f32[4,16,4096]{1,0,2:T(4,128)} fusion(bf16[4,32,4096]{1,0,2:T(4,128)(2,1)} %copy.34, f32[32]{0:T(128)S(1)} %subtract_negate_fusion, f32[16,4096]{0,1:T(8,128)S(1)} %copy.31), kind=kOutput, calls=%fused_computation.19 | convolution fusion | flops 102760448 | bytes 2359424 | tf_op jit(solution)/shard_map/tkd,ntd->nkd/dot_general | solution.py:60
  50.4 7.6 %copy.36 = f32[4,16,4096]{2,1,0:T(8,128)} copy(f32[4,16,4096]{1,0,2:T(4,128)} %fusion.13) | data formatting | bytes 2097152
  58.0 7.5 %while.27 = (s32[]{:T(128)}, f32[16,4096]{1,0:T(8,128)S(1)}, f32[4,16,4096]{2,1,0:T(8,128)}, f32[16,4096]{1,0:T(8,128)S(1)}, f32[4,16,4096]{2,1,0:T(8,128)}, /*index=5*/s32[]{:T(128)}, s32[]{:T(128)}) while((s32[]{:T(128)}, f32[16,4096]{1,0:T(8,128)S(1)}, f32[4,16,4096]{2,1,0:T(8,128)}, f32[16,4096]{1,0:T(8,128)S(1)}, ...), condition=%wide.region_2.3_spmd.clone, body=%wide.region_1.2_spmd.clone.sunk | while | flops 262147 | bytes 1572968 | solution.py:68
  66.2 6.0 %stack.2 = bf16[32,128,2048]{2,1,0:T(8,128)(2,1)} broadcast(bf16[128,2048]{1,0:T(8,128)(2,1)S(1)} %copy-done.2), dimensions={1,2} | broadcast | bytes 17301504 | tf_op jit(solution)/shard_map/stack | solution.py:13
  72.3 7.6 %all-to-all-start = ((bf16[32,128,2048]{2,1,0:T(8,128)(2,1)}), bf16[32,128,2048]{2,1,0:T(8,128)(2,1)}, u32[]{:S(2)}, u32[]{:S(2)}) async-start(bf16[32,128,2048]{2,1,0:T(8,128)(2,1)} %stack.2), calls=%async_computation | async-start | bytes 33554432 | tf_op jit(solution)/shard_map/all_to_all | solution.py:13
  79.9 2.0 copy.30
  81.9 25.7 %multiply_reduce_fusion = bf16[32,4096]{0,1:T(8,128)(2,1)} fusion(f32[16,4096]{0,1:T(8,128)S(1)} %copy.31, f32[32]{0:T(128)S(1)} %iota_negate_fusion, f32[16,4096]{0,1:T(8,128)} %copy.30), kind=kLoop, calls=%fused_computation.12 | loop fusion | flops 6160384 | bytes 786560 | tf_op jit(solution)/shard_map/reduce_sum | solution.py:43
  107.5 1.5 copy.32
  109.1 5.6 %fusion.20 = bf16[4096,32,32]{0,2,1:T(8,128)(2,1)} fusion(s32[32,32]{1,0:T(8,128)S(1)} %iota_subtract_fusion, bf16[32,4096]{1,0:T(8,128)(2,1)S(1)} %copy.32), kind=kOutput, calls=%fused_computation.26 | convolution fusion | flops 268468224 | bytes 8654848 | tf_op jit(solution)/shard_map/dot_general | solution.py:53
  114.7 44.1 %copy.33 = bf16[4096,32,32]{2,1,0:T(8,128)(2,1)} copy(bf16[4096,32,32]{0,2,1:T(8,128)(2,1)} %fusion.20) | data formatting | bytes 16777216 | tf_op jit(solution)/shard_map/dot_general | solution.py:53
  158.9 22.7 %fusion.24 = f32[4096,32,4]{1,2,0:T(4,128)} fusion(bf16[4096,32,32]{2,1,0:T(8,128)(2,1)} %copy.33, bf16[4,32,4096]{1,0,2:T(4,128)(2,1)} %copy.34), kind=kOutput, calls=%fused_computation.38 | convolution fusion | flops 33554432 | bytes 11534336 | tf_op jit(solution)/shard_map/dts,nsd->ntd/dot_general | solution.py:57
  181.6 143.5 %all-gather.7.cloned.1.call-done = f32[512,4096]{1,0:T(8,128)} async-done(((f32[16,4096]{1,0:T(8,128)}), f32[512,4096]{1,0:T(8,128)}) %all-gather.7.cloned.1.call-update) | async-done | bytes 8388624 | tf_op jit(solution)/shard_map/all_gather | solution.py:23
  325.1 39.4 %while.28 = (s32[]{:T(128)}, f32[16,4096]{1,0:T(8,128)S(1)}, s32[]{:T(128)}, f32[32,16,4096]{2,1,0:T(8,128)}, f32[32,16,4096]{2,1,0:T(8,128)}, /*index=5*/s32[]{:T(128)}, s32[]{:T(128)}) while((s32[]{:T(128)}, f32[16,4096]{1,0:T(8,128)S(1)}, s32[]{:T(128)}, f32[32,16,4096]{2,1,0:T(8,128)}, f32[32,16,4096]{2,1,0:T(8,128)}, ...), condition=%wide.region_4.5_spmd.clone, body=%wide.region_3.4_spmd.clone.sunk | while | flops 262148 | bytes 1048685 | solution.py:32
  331.4 1.2 fusion.35
  364.5 2.5 multiply_add_fusion
  367.0 6.9 %copy.37 = f32[4,16,4096]{1,0,2:T(4,128)} copy(f32[4,16,4096]{2,1,0:T(8,128)} %multiply_add_fusion) | data formatting | bytes 2097152 | tf_op jit(solution)/shard_map/add | solution.py:79
  374.0 47.3 %bitcast_add_fusion.2 = f32[4,32,4096]{1,0,2:T(4,128)} fusion(f32[4096,32,4]{1,2,0:T(4,128)} %fusion.24, f32[4,16,4096]{1,0,2:T(4,128)} %copy.37, f32[32]{0:T(128)S(1)} %add_negate_fusion, f32[16,4096]{0,1:T(8,128)S(1)} %copy.31, f32[16,4096]{0,1:T(8,128)} %copy.30), kind=kOutput, calls=%fused_computation.18 | convolution fusion | flops 105381888 | bytes 5767296 | tf_op jit(solution)/shard_map/tkd,nkd->ntd/dot_general | solution.py:83
  421.3 7.0 %copy.38 = f32[4,32,4096]{2,1,0:T(8,128)S(1)} copy(f32[4,32,4096]{1,0,2:T(4,128)} %bitcast_add_fusion.2) | data formatting | bytes 4194304 | tf_op jit(solution)/shard_map/add | solution.py:84
  428.3 2.1 fusion.19
  430.3 62.8 %all-to-all-done = bf16[32,128,2048]{2,1,0:T(8,128)(2,1)} async-done(((bf16[32,128,2048]{2,1,0:T(8,128)(2,1)}), bf16[32,128,2048]{2,1,0:T(8,128)(2,1)}, u32[]{:S(2)}, u32[]{:S(2)}) %all-to-all-start) | async-done | bytes 16777248 | tf_op jit(solution)/shard_map/all_to_all | solution.py:13
  493.1 8.9 %convolution_convert_fusion = bf16[128,2048]{1,0:T(8,128)(2,1)} fusion(bf16[128,4096]{1,0:T(8,128)(2,1)S(1)} %fusion.19, bf16[4096,2048]{1,0:T(8,128)(2,1)} %bitcast.10), kind=kOutput, calls=%fused_computation.20 | convolution fusion | flops 2147745792 | bytes 18350080 | tf_op jit(solution)/shard_map/dot_general | solution.py:89
  (59 shorter events, 45.7 us)
Async XLA Ops:
  6.5 175.0 %all-gather.5.cloned.1.call-start = ((), (), s32[]{:S(2)}) async-start(), calls=%async_computation.1 | async-start | bytes 8650752 | tf_op jit(solution)/shard_map/all_gather | solution.py:23
  8.5 316.6 %all-gather.7.cloned.1.call-start = ((), (), s32[]{:S(2)}) async-start(), calls=%async_computation.2 | async-start | bytes 8650752 | tf_op jit(solution)/shard_map/all_gather | solution.py:23
  50.4 15.8 %copy-start.2 = (bf16[128,2048]{1,0:T(8,128)(2,1)S(1)}, bf16[128,2048]{1,0:T(8,128)(2,1)}, u32[]{:S(2)}) copy-start(bf16[128,2048]{1,0:T(8,128)(2,1)} %param.15) | copy-start | bytes 1572868
  65.5 0.7 copy-start
  72.3 420.8 %all-to-all-start = ((bf16[32,128,2048]{2,1,0:T(8,128)(2,1)}), bf16[32,128,2048]{2,1,0:T(8,128)(2,1)}, u32[]{:S(2)}, u32[]{:S(2)}) async-start(bf16[32,128,2048]{2,1,0:T(8,128)(2,1)} %stack.2), calls=%async_computation | async-start | bytes 33554432 | tf_op jit(solution)/shard_map/all_to_all | solution.py:13
  158.8 205.6 %copy-start.1 = (f32[4096,16]{0,1:T(8,128)S(1)}, f32[4096,16]{0,1:T(8,128)}, u32[]{:S(2)}) copy-start(f32[4096,16]{0,1:T(8,128)} %param.12) | copy-start | bytes 786436
  421.3 7.0 %copy-start.3 = (f32[4096]{0:T(1024)S(1)}, f32[4096]{0:T(1024)}, u32[]{:S(2)}) copy-start(f32[4096]{0:T(1024)} %param.14) | copy-start | bytes 49156
Sparse Core Ops, SparseCore 0:
  10.2 82.8 all-gather.4
  96.0 229.0 all-gather.6
